TPU v7x, 32 devices: a whole 2x2x4 slice. The times are simulated.
32 devices in a mesh: dp: 4 (over y, x), seq: 8 (over z, core).
Axes of the slice: x: 2, y: 2, z: 4, core: 2. Of those that a mesh axis runs over, the one named last changes fastest.
Arguments:
- layer_in: float32 [4096, 2048], P(('dp', 'seq')), may hold values from -6 to 6
- norm1_gain: float32 [2048], replicated, may hold values from 0.25 to 1.75
- qkv_weight: bfloat16 [2048, 6144], P('dp'), may hold values from -0.79549513 to 0.79549513
- out_weight: bfloat16 [2048, 2048], P('dp'), may hold values from -2 to 2
- norm2_gain: float32 [2048], replicated, may hold values from 0.25 to 1.75
- gate_up_weight: bfloat16 [2048, 16384], P('dp'), may hold values from -0.125 to 0.125
- down_weight: bfloat16 [2048, 8192], P('dp'), may hold values from -0.0625 to 0.0625
- cotangent: float32 [4096, 2048], P(('dp', 'seq')), may hold values from -6 to 6
Outputs:
- layer_out: float32 [4096, 2048], P(('dp', 'seq'))
- input_grad: float32 [4096, 2048], P(('dp', 'seq'))
- norm1_grad: float32 [2048], P(('dp', 'seq'))
- qkv_grad: float32 [2048, 6144], P(('dp', 'seq'))
- out_grad: float32 [2048, 2048], P(('dp', 'seq'))
- norm2_grad: float32 [2048], P(('dp', 'seq'))
- gate_up_grad: float32 [2048, 16384], P(('dp', 'seq'))
- down_grad: float32 [2048, 8192], P(('dp', 'seq'))
All inputs are finite; a program needn't handle non-finite values.
Results may differ from a plain program's by a relative error of at most 0.018.
Values may be sent and summed in bfloat16 or wider, within the bound.
No kernel may reach another device: no remote copies, remote signals or barrier semaphores. Data moves between devices by JAX's collectives and lax.ppermute only.
A program may use at most 384 MiB of HBM per device.

v0:
```python
import jax
import jax.numpy as jnp
from jax import lax
from jax.sharding import PartitionSpec as P

HD = 64
EPS = 1e-05
THETA = 130000.0


def rotary_tables(length, head_dim):
    half_dim = head_dim // 2
    inverse = THETA ** (-(jnp.arange(half_dim).astype(jnp.float32) * 2.0) / head_dim)
    angles = jnp.arange(length).astype(jnp.float32)[:, None] * inverse[None, :]
    cosine = jnp.cos(angles)
    sine = jnp.sin(angles)
    return (jnp.concatenate([cosine, cosine], 1), jnp.concatenate([sine, sine], 1))


def rotate(values, cosine, sine):
    half_dim = values.shape[-1] // 2
    turned = jnp.concatenate([-values[..., half_dim:], values[..., :half_dim]], -1)
    return values * cosine[:, None, :] + turned * sine[:, None, :]


def scores_for(queries, key_rot, first_row, length, score_scale):
    block_rows = queries.shape[0]
    raw_scores = (
        jnp.einsum("qhd,khd->hqk", queries, key_rot, preferred_element_type=jnp.float32)
        * score_scale
    )
    query_pos = first_row + jnp.arange(block_rows)
    key_pos = jnp.arange(length)
    allowed = key_pos[None, :] <= query_pos[:, None]
    return jnp.where(allowed[None], raw_scores, -1e30)


def attend_forward(query_rot, key_rot, value_heads):
    length, head_count, head_dim = query_rot.shape
    block_rows = min(512, length)
    score_scale = head_dim ** (-0.5)

    def one_block(block_index):
        first_row = block_index * block_rows
        queries = lax.dynamic_slice_in_dim(query_rot, first_row, block_rows, 0)
        scores = scores_for(queries, key_rot, first_row, length, score_scale)
        row_max = jnp.max(scores, axis=2, keepdims=True)
        row_total = jnp.sum(jnp.exp(scores - row_max), axis=2, keepdims=True)
        log_total = row_max + jnp.log(row_total)
        prob_low = jnp.exp(scores - log_total).astype(jnp.bfloat16)
        mixed = jnp.einsum(
            "hqk,khd->qhd", prob_low, value_heads, preferred_element_type=jnp.float32
        )
        return (mixed.astype(jnp.bfloat16), log_total[:, :, 0])

    mixed, log_total = lax.map(one_block, jnp.arange(length // block_rows))
    return (mixed.reshape(length, head_count, head_dim), log_total)


def attend_backward(query_rot, key_rot, value_heads, mixed, log_total, grad_mixed):
    length, head_count, head_dim = query_rot.shape
    block_rows = min(512, length)
    score_scale = head_dim ** (-0.5)
    row_delta = jnp.sum(grad_mixed.astype(jnp.float32) * mixed.astype(jnp.float32), axis=2)

    def one_block(carry, block_index):
        grad_keys, grad_values = carry
        first_row = block_index * block_rows
        queries = lax.dynamic_slice_in_dim(query_rot, first_row, block_rows, 0)
        grad_rows = lax.dynamic_slice_in_dim(grad_mixed, first_row, block_rows, 0)
        delta_rows = lax.dynamic_slice_in_dim(row_delta, first_row, block_rows, 0)
        scores = scores_for(queries, key_rot, first_row, length, score_scale)
        probs = jnp.exp(scores - log_total[block_index][:, :, None])
        prob_low = probs.astype(jnp.bfloat16)
        grad_values = grad_values + jnp.einsum(
            "hqk,qhd->khd", prob_low, grad_rows, preferred_element_type=jnp.float32
        )
        grad_probs = jnp.einsum(
            "qhd,khd->hqk", grad_rows, value_heads, preferred_element_type=jnp.float32
        )
        grad_scores = (score_scale * probs * (grad_probs - delta_rows.T[:, :, None])).astype(
            jnp.bfloat16
        )
        grad_queries = jnp.einsum(
            "hqk,khd->qhd", grad_scores, key_rot, preferred_element_type=jnp.float32
        )
        grad_keys = grad_keys + jnp.einsum(
            "hqk,qhd->khd", grad_scores, queries, preferred_element_type=jnp.float32
        )
        return ((grad_keys, grad_values), grad_queries)

    empty = jnp.zeros((length, head_count, head_dim), jnp.float32)
    (grad_keys, grad_values), grad_queries = lax.scan(
        one_block, (empty, empty), jnp.arange(length // block_rows)
    )
    return (grad_queries.reshape(length, head_count, head_dim), grad_keys, grad_values)


def norm_backward(grad_normed, normed, gain, inv_rms):
    grad_hat = grad_normed * gain
    return inv_rms * (grad_hat - normed * jnp.mean(grad_hat * normed, axis=1, keepdims=True))


def keep_step(source, weight_piece):
    running = jnp.dot(source, weight_piece, preferred_element_type=jnp.float32)
    return (running, weight_piece)


def keep_columns(source, weight_piece):
    partial_out = jnp.einsum("tf,rf->tr", source, weight_piece, preferred_element_type=jnp.float32)
    return (partial_out, weight_piece)


def row_product(left, right):
    return jnp.einsum("tr,tc->rc", left, right, preferred_element_type=jnp.float32)


def heads_from_tokens(token_block):
    gathered = lax.all_to_all(token_block, "seq", split_axis=2, concat_axis=0, tiled=True)
    return gathered.reshape(gathered.shape[0], gathered.shape[1], gathered.shape[3] // HD, HD)


def tokens_from_heads(head_block):
    row_total = head_block.shape[0]
    flattened = head_block.reshape(row_total, head_block.shape[1], 1, head_block.shape[2] * HD)
    return lax.all_to_all(flattened, "seq", split_axis=0, concat_axis=2, tiled=True)


def seq_major(rows_side, dp_count, group_count, shard_rows):
    token_rows = rows_side.shape[0]
    reordered = rows_side.reshape(token_rows, dp_count, group_count, shard_rows).transpose(
        0, 2, 1, 3
    )
    return reordered.reshape(token_rows, dp_count * group_count * shard_rows)


def shards(
    layer_in, norm1_gain, qkv_weight, out_weight, norm2_gain, gate_up_weight, down_weight, cotangent
):
    token_rows, model_width = layer_in.shape
    group_count = lax.axis_size("seq")
    dp_count = lax.axis_size("dp")
    group_width = model_width // group_count
    hidden_units = down_weight.shape[1]
    length = token_rows * group_count
    shard_rows = model_width // (dp_count * group_count)
    inv_rms1 = lax.rsqrt(jnp.mean(layer_in * layer_in, axis=1, keepdims=True) + EPS)
    normed1 = layer_in * inv_rms1
    xn_first = (normed1 * norm1_gain).astype(jnp.bfloat16)
    qkv_sum, qkv_full = keep_step(xn_first, lax.all_gather(qkv_weight, "dp", axis=0, tiled=True))
    qkv_low = qkv_sum.astype(jnp.bfloat16).reshape(token_rows, 3, group_count, group_width)
    head_qkv = heads_from_tokens(qkv_low)
    cosine, sine = rotary_tables(length, HD)
    query_rot = rotate(head_qkv[:, 0].astype(jnp.float32), cosine, sine).astype(jnp.bfloat16)
    key_rot = rotate(head_qkv[:, 1].astype(jnp.float32), cosine, sine).astype(jnp.bfloat16)
    value_heads = head_qkv[:, 2]
    mixed, log_total = attend_forward(query_rot, key_rot, value_heads)
    local_heads = mixed.shape[1]
    token_mixed = tokens_from_heads(mixed.reshape(length, 1, local_heads, HD))
    attn_low = token_mixed.reshape(token_rows, model_width)
    attn_sum, out_full = keep_step(attn_low, lax.all_gather(out_weight, "dp", axis=0, tiled=True))
    hidden_res = layer_in + attn_sum
    inv_rms2 = lax.rsqrt(jnp.mean(hidden_res * hidden_res, axis=1, keepdims=True) + EPS)
    normed2 = hidden_res * inv_rms2
    xn_second = (normed2 * norm2_gain).astype(jnp.bfloat16)
    gate_up, gate_up_full = keep_step(
        xn_second, lax.all_gather(gate_up_weight, "dp", axis=0, tiled=True)
    )
    gate = gate_up[:, :hidden_units]
    up_part = gate_up[:, hidden_units:]
    sigmoid_gate = jax.nn.sigmoid(gate)
    act_low = (gate * sigmoid_gate * up_part).astype(jnp.bfloat16)
    mlp_out, down_full = keep_columns(
        act_low, lax.all_gather(down_weight, "dp", axis=0, tiled=True)
    )
    layer_out = hidden_res + mlp_out
    grad_low = cotangent.astype(jnp.bfloat16)
    grad_act = jnp.dot(grad_low, down_full, preferred_element_type=jnp.float32)
    grad_gate = grad_act * up_part * sigmoid_gate * (1.0 + gate * (1.0 - sigmoid_gate))
    grad_up = grad_act * gate * sigmoid_gate
    grad_gate_up = jnp.concatenate([grad_gate, grad_up], 1).astype(jnp.bfloat16)
    grad_xn2 = jnp.einsum(
        "tc,rc->tr", grad_gate_up, gate_up_full, preferred_element_type=jnp.float32
    )
    norm2_term = jnp.sum(grad_xn2 * normed2, axis=0)
    grad_hidden = cotangent + norm_backward(grad_xn2, normed2, norm2_gain, inv_rms2)
    hidden_low = grad_hidden.astype(jnp.bfloat16)
    grad_attn = jnp.einsum(
        "tc,rc->tr", hidden_low, out_full, preferred_element_type=jnp.float32
    ).astype(jnp.bfloat16)
    grad_heads = heads_from_tokens(grad_attn.reshape(token_rows, 1, group_count, group_width))
    grad_mixed = grad_heads[:, 0]
    grad_query, grad_key, grad_value = attend_backward(
        query_rot, key_rot, value_heads, mixed, log_total, grad_mixed
    )
    grad_query = rotate(grad_query, cosine, -sine)
    grad_key = rotate(grad_key, cosine, -sine)
    grad_stack = jnp.stack([grad_query, grad_key, grad_value], 1).astype(jnp.bfloat16)
    token_grads = tokens_from_heads(grad_stack)
    grad_qkv = token_grads.reshape(token_rows, 3 * model_width)
    grad_xn1 = jnp.einsum("tc,rc->tr", grad_qkv, qkv_full, preferred_element_type=jnp.float32)
    norm1_term = jnp.sum(grad_xn1 * normed1, axis=0)
    input_grad = grad_hidden + norm_backward(grad_xn1, normed1, norm1_gain, inv_rms1)
    norm_grads = (
        lax.psum_scatter(norm1_term, ("dp", "seq"), scatter_dimension=0, tiled=True),
        lax.psum_scatter(norm2_term, ("dp", "seq"), scatter_dimension=0, tiled=True),
    )
    widths = (3 * model_width, model_width, 2 * hidden_units, hidden_units)
    gathered_rows = (
        lax.all_gather(
            seq_major(xn_first, dp_count, group_count, shard_rows), "dp", axis=0, tiled=True
        ),
        lax.all_gather(
            seq_major(attn_low, dp_count, group_count, shard_rows), "dp", axis=0, tiled=True
        ),
        lax.all_gather(
            seq_major(xn_second, dp_count, group_count, shard_rows), "dp", axis=0, tiled=True
        ),
        lax.all_gather(
            seq_major(grad_low, dp_count, group_count, shard_rows), "dp", axis=0, tiled=True
        ),
    )
    split_cols = (
        lax.all_to_all(grad_qkv, "dp", split_axis=1, concat_axis=0, tiled=True),
        lax.all_to_all(hidden_low, "dp", split_axis=1, concat_axis=0, tiled=True),
        lax.all_to_all(grad_gate_up, "dp", split_axis=1, concat_axis=0, tiled=True),
        lax.all_to_all(act_low, "dp", split_axis=1, concat_axis=0, tiled=True),
    )
    stripes = lax.psum_scatter(
        jnp.concatenate(
            [row_product(gathered_rows[which], split_cols[which]) for which in range(4)], 1
        ).astype(jnp.bfloat16),
        "seq",
        scatter_dimension=0,
        tiled=True,
    ).astype(jnp.float32)
    owned_rows = (
        lax.all_to_all(stripes.astype(jnp.bfloat16), "dp", split_axis=0, concat_axis=1, tiled=True)
        .astype(stripes.dtype)
        .reshape(shard_rows, dp_count, -1)
    )
    pieces = []
    offset = 0
    for column_width in widths:
        share_cols = column_width // dp_count
        pieces.append(
            owned_rows[:, :, offset : offset + share_cols].reshape(shard_rows, column_width)
        )
        offset = offset + share_cols
    return (
        layer_out,
        input_grad,
        norm_grads[0],
        pieces[0],
        pieces[1],
        norm_grads[1],
        pieces[2],
        pieces[3],
    )


def solution(mesh):
    in_specs = (
        P(("dp", "seq"), None),
        P(),
        P("dp", None),
        P("dp", None),
        P(),
        P("dp", None),
        P("dp", None),
        P(("dp", "seq"), None),
    )
    out_specs = (
        P(("dp", "seq"), None),
        P(("dp", "seq"), None),
        P(("dp", "seq")),
        P(("dp", "seq"), None),
        P(("dp", "seq"), None),
        P(("dp", "seq")),
        P(("dp", "seq"), None),
        P(("dp", "seq"), None),
    )
    return jax.shard_map(shards, mesh=mesh, in_specs=in_specs, out_specs=out_specs, check_vma=False)
```

profile of v0, /device:TPU:0, one launch (start us, length us, event | category | flops | bytes accessed | tf_op | source)
XLA Modules:
  0.0 2005.1 jit_solution(732256753957964172)
XLA Ops:
  11.0 229.2 %all-gather.9.cloned.1.call-done = bf16[2048,6144]{1,0:T(8,128)(2,1)} async-done(((bf16[512,6144]{1,0:T(8,128)(2,1)}), bf16[2048,6144]{1,0:T(8,128)(2,1)}) %all-gather.9.cloned.1.call-update) | async-done | bytes 25165840 | tf_op jit(solution)/shard_map/all_gather | solution.py:150
  240.2 11.6 convolution_convert_fusion.2
  253.7 4.9 all-to-all-start
  260.0 36.4 %all-to-all-done = bf16[128,3,8,256]{3,0,1,2:T(8,128)(2,1)} async-done(((bf16[128,3,8,256]{3,0,1,2:T(8,128)(2,1)}), bf16[128,3,8,256]{3,0,1,2:T(8,128)(2,1)}, u32[]{:S(2)}, u32[]{:S(2)}) %all-to-all-start) | async-done | bytes 1572896 | tf_op jit(solution)/shard_map/all_to_all | solution.py:119
  306.0 16.1 while.27
  341.1 12.1 all-to-all-done.1
  357.7 7.2 multiply_reduce_fusion.5
  366.7 541.4 %all-gather.13.cloned.1.call-done = bf16[2048,16384]{1,0:T(8,128)(2,1)} async-done(((bf16[512,16384]{1,0:T(8,128)(2,1)}), bf16[2048,16384]{1,0:T(8,128)(2,1)}) %all-gather.13.cloned.1.call-update) | async-done | bytes 67108880 | tf_op jit(solution)/shard_map/all_gather | solution.py:167
  908.1 34.6 %fusion.51 = f32[128,16384]{1,0:T(8,128)} fusion(bf16[128,2048]{1,0:T(8,128)(2,1)S(1)} %multiply_convert_fusion.4, bf16[2048,16384]{1,0:T(8,128)(2,1)} %all-gather.13.cloned.1.call-done), kind=kOutput, calls=%fused_computation.121 | convolution fusion | flops 8589934592 | bytes 76021760 | tf_op jit(solution)/shard_map/dot_general | solution.py:105
  942.7 264.2 %all-gather.15.cloned.1.call-done = bf16[2048,8192]{1,0:T(8,128)(2,1)} async-done(((bf16[512,8192]{1,0:T(8,128)(2,1)}), bf16[2048,8192]{1,0:T(8,128)(2,1)}) %all-gather.15.cloned.1.call-update) | async-done | bytes 33554448 | tf_op jit(solution)/shard_map/all_gather | solution.py:174
  1206.9 19.6 multiply_convert_fusion.2
  1226.5 30.7 %multiply_reduce_fusion = (f32[2048]{0:T(1024)}, f32[128]{0:T(128)S(1)}, f32[128,2048]{1,0:T(8,128)}) fusion(f32[128,2048]{1,0:T(8,128)S(1)} %copy-done.4, f32[128]{0:T(128)S(1)} %add_rsqrt_fusion, f32[2048]{0:T(1024)S(1)} %copy-done.24, bf16[2048,16384]{1,0:T(8,128)(2,1)} %all-gather.13.cloned.1.call-done, bf16[128,8192]{1,0:T(8,128)(2,1)} %get-tuple-element.206, ...), kind=kOutput, calls=%fused_computation.84 | convolution fusion | flops 8599894016 | bytes 73417728 | tf_op jit(solution)/shard_map/tc,rc->tr/dot_general | solution.py:182
  1260.1 6.3 convolution_convert_fusion.4
  1273.7 13.6 all-to-all-done.2
  1306.3 72.6 %while.28 = (s32[]{:T(128)}, f32[1024,4,64]{0,2,1:T(8,128)S(1)}, f32[1024,4,64]{0,2,1:T(8,128)}, f32[2,512,4,64]{1,0,3,2:T(2,128)}, s32[2]{0:T(128)S(1)}, /*inde...) while((s32[]{:T(128)}, f32[1024,4,64]{0,2,1:T(8,128)S(1)}, ...), condition=%wide.region_9.10_spmd.clone, body=%wide.region_8.9_spmd.clone.sunk | while | flops 1366819328 | bytes 107540888 | solution.py:93
  1314.5 7.1 multiply_convert_fusion.7
  1332.2 10.4 dynamic_update_slice.20
  1350.8 7.1 multiply_convert_fusion.7
  1368.5 10.4 dynamic_update_slice.20
  1402.4 43.3 %all-to-all-done.3 = bf16[1024,3,1,256]{3,1,2,0:T(4,128)(2,1)} async-done(((bf16[1024,3,1,256]{3,1,2,0:T(4,128)(2,1)}), bf16[1024,3,1,256]{3,1,2,0:T(4,128)(2,1)}, u32[]{:S(2)}, u32[]{:S(2)}) %all-to-all-start.3) | async-done | bytes 1572896 | tf_op jit(solution)/shard_map/all_to_all | solution.py:126
  1445.7 4.9 all-to-all-start.6
  1459.0 10.3 convert_bitcast_fusion.1
  1474.8 40.3 %all-to-all-done.6 = bf16[128,4,4096]{2,0,1:T(8,128)(2,1)} async-done(((bf16[128,4,4096]{2,0,1:T(8,128)(2,1)}), bf16[128,4,4096]{2,0,1:T(8,128)(2,1)}, u32[]{:S(2)}, u32[]{:S(2)}) %all-to-all-start.6) | async-done | bytes 4194336 | tf_op jit(solution)/shard_map/all_to_all | solution.py:226
  1519.8 14.9 convolution_convert_fusion
  1539.5 8.2 convolution_convert_fusion.1
  1547.7 8.6 copy.149
  1556.3 22.2 %pad_maximum_fusion = bf16[2048,8192]{1,0:T(8,128)(2,1)} fusion(bf16[2048,2048]{1,0:T(8,128)(2,1)} %convert_bitcast_fusion.1, bf16[2048,4096]{1,0:T(8,128)(2,1)} %convolution_convert_fusion, bf16[2048,512]{1,0:T(8,128)(2,1)S(1)} %copy.150, bf16[2048,1536]{1,0:T(8,128)(2,1)} %copy.149), kind=kLoop, calls=%fused_computation.43 | loop fusion | flops 134217728 | bytes 67108864 | tf_op jit(solution)/shard_map/concatenate | solution.py:230
  1578.6 323.2 %reduce-scatter.2.cloned.1.call-done = bf16[256,8192]{1,0:T(8,128)(2,1)} async-done(((bf16[2048,8192]{1,0:T(8,128)(2,1)}), bf16[256,8192]{1,0:T(8,128)(2,1)}) %reduce-scatter.2.cloned.1.call-update) | async-done | bytes 4194320 | tf_op jit(solution)/shard_map/reduce_scatter | solution.py:229
  1901.7 5.3 all-to-all-start.8
  1907.1 17.4 convolution_add_fusion
  1924.5 13.8 multiply_reduce_fusion.1
  1938.3 47.7 %all-reduce.2 = (f32[2048]{0:T(1024)S(1)}, f32[2048]{0:T(1024)S(1)}) all-reduce(f32[2048]{0:T(1024)S(1)} %get-tuple-element.159, f32[2048]{0:T(1024)S(1)} %copy-done.25), channel_id=2, replica_groups=mesh['dp'=4,'seq'=8] {'dp','seq'}, use_global_device_ids=true, to_apply=%region_12.13.clone | all-reduce | flops 4096 | bytes 32768
  (216 shorter events, 176.4 us)
Async XLA Ops:
  7.2 233.0 %all-gather.9.cloned.1.call-start = ((), (), s32[]{:S(2)}) async-start(), calls=%async_computation.10 | async-start | bytes 31457280 | tf_op jit(solution)/shard_map/all_gather | solution.py:150
  7.9 349.8 %all-gather.11.cloned.1.call-start = ((), (), s32[]{:S(2)}) async-start(), calls=%async_computation.11 | async-start | bytes 10485760 | tf_op jit(solution)/shard_map/all_gather | solution.py:161
  8.6 899.4 %all-gather.13.cloned.1.call-start = ((), (), s32[]{:S(2)}) async-start(), calls=%async_computation.12 | async-start | bytes 83886080 | tf_op jit(solution)/shard_map/all_gather | solution.py:167
  9.4 1197.5 %all-gather.15.cloned.1.call-start = ((), (), s32[]{:S(2)}) async-start(), calls=%async_computation.13 | async-start | bytes 41943040 | tf_op jit(solution)/shard_map/all_gather | solution.py:174
  10.8 241.0 %copy-start.26 = (f32[128]{0:T(128)}, f32[128]{0:T(128)S(1)}, u32[]{:S(2)}) copy-start(f32[128]{0:T(128)S(1)} %add_rsqrt_fusion.1) | copy-start | bytes 1540
  11.0 240.8 %copy-start.9 = (bf16[128,2048]{1,0:T(8,128)(2,1)}, bf16[128,2048]{1,0:T(8,128)(2,1)S(1)}, u32[]{:S(2)}) copy-start(bf16[128,2048]{1,0:T(8,128)(2,1)S(1)} %multiply_convert_fusion.5) | copy-start | bytes 1572868
  253.7 42.7 %all-to-all-start = ((bf16[128,3,8,256]{3,0,1,2:T(8,128)(2,1)}), bf16[128,3,8,256]{3,0,1,2:T(8,128)(2,1)}, u32[]{:S(2)}, u32[]{:S(2)}) async-start(bf16[128,3,8,256]{3,0,1,2:T(8,128)(2,1)} %copy.121), calls=%async_computation | async-start | bytes 3145728 | tf_op jit(solution)/shard_map/all_to_all | solution.py:119
  259.2 46.4 %copy-start.11 = (f32[1024,64]{0,1:T(8,128)}, f32[1024,64]{0,1:T(8,128)S(1)}, u32[]{:S(2)}) copy-start(f32[1024,64]{0,1:T(8,128)S(1)} %pad_maximum_fusion.4) | copy-start | bytes 786436
  322.1 19.0 copy-start.16
  334.5 18.8 all-to-all-start.1
  338.0 1113.8 %all-gather.19.cloned.1.call-start = ((), (), s32[]{:S(2)}) async-start(), calls=%async_computation.15 | async-start | bytes 2621440 | tf_op jit(solution)/shard_map/all_gather | solution.py:213
  357.7 7.3 copy-start.24
  366.7 840.2 %copy-start.17 = (bf16[128,2048]{0,1:T(8,128)(2,1)S(1)}, bf16[128,2048]{0,1:T(8,128)(2,1)}, u32[]{:S(2)}) copy-start(bf16[128,2048]{0,1:T(8,128)(2,1)} %copy.126) | copy-start | bytes 1572868
  942.7 283.8 %copy-start.4 = (f32[128,2048]{1,0:T(8,128)S(1)}, f32[128,2048]{1,0:T(8,128)}, u32[]{:S(2)}) copy-start(f32[128,2048]{1,0:T(8,128)} %get-tuple-element.226) | copy-start | bytes 3145732
  1260.1 11.9 copy-start.18
  1267.4 19.9 all-to-all-start.2
  1271.9 187.1 %all-gather.23.cloned.1.call-start = ((), (), s32[]{:S(2)}) async-start(), calls=%async_computation.17 | async-start | bytes 2621440 | tf_op jit(solution)/shard_map/all_gather | solution.py:219
  1287.4 14.3 all-to-all-start.5
  1301.7 90.6 %all-to-all-start.7 = ((bf16[128,4,2048]{2,0,1:T(8,128)(2,1)}), bf16[128,4,2048]{2,0,1:T(8,128)(2,1)}, u32[]{:S(2)}, u32[]{:S(2)}) async-start(bf16[128,4,2048]{2,0,1:T(8,128)(2,1)} %bitcast.225), calls=%async_computation.7 | async-start | bytes 4194304 | tf_op jit(solution)/shard_map/all_to_all | solution.py:227
  1392.3 53.4 %all-to-all-start.3 = ((bf16[1024,3,1,256]{3,1,2,0:T(4,128)(2,1)}), bf16[1024,3,1,256]{3,1,2,0:T(4,128)(2,1)}, u32[]{:S(2)}, u32[]{:S(2)}) async-start(bf16[1024,3,1,256]{3,1,2,0:T(4,128)(2,1)} %copy.132), calls=%async_computation.3 | async-start | bytes 4194304 | tf_op jit(solution)/shard_map/all_to_all | solution.py:126
  1396.7 123.1 %all-gather.21.cloned.1.call-start = ((), (), s32[]{:S(2)}) async-start(), calls=%async_computation.16 | async-start | bytes 2621440 | tf_op jit(solution)/shard_map/all_gather | solution.py:216
  1402.4 48.2 %copy-start.10 = (bf16[128,2048]{1,0:T(8,128)(2,1)S(1)}, bf16[128,2048]{1,0:T(8,128)(2,1)}, u32[]{:S(2)}) copy-start(bf16[128,2048]{1,0:T(8,128)(2,1)} %copy-done.9) | copy-start | bytes 1572868
  1445.7 69.4 %all-to-all-start.6 = ((bf16[128,4,4096]{2,0,1:T(8,128)(2,1)}), bf16[128,4,4096]{2,0,1:T(8,128)(2,1)}, u32[]{:S(2)}, u32[]{:S(2)}) async-start(bf16[128,4,4096]{2,0,1:T(8,128)(2,1)} %pad_maximum_fusion.1), calls=%async_computation.6 | async-start | bytes 8388608 | tf_op jit(solution)/shard_map/all_to_all | solution.py:226
  1450.6 89.0 %all-gather.17.cloned.1.call-start = ((), (), s32[]{:S(2)}) async-start(), calls=%async_computation.14 | async-start | bytes 2621440 | tf_op jit(solution)/shard_map/all_gather | solution.py:210
  1515.1 21.9 %all-to-all-start.4 = ((bf16[128,4,1536]{0,2,1:T(8,128)(2,1)}), bf16[128,4,1536]{0,2,1:T(8,128)(2,1)}, u32[]{:S(2)}, u32[]{:S(2)}) async-start(bf16[128,4,1536]{0,2,1:T(8,128)(2,1)} %bitcast.30), calls=%async_computation.4 | async-start | bytes 3145728 | tf_op jit(solution)/shard_map/all_to_all | solution.py:224
  1519.4 382.3 %reduce-scatter.2.cloned.1.call-start = ((), (), s32[]{:S(2)}) async-start(), calls=%async_computation.18 | async-start | bytes 37748736 | tf_op jit(solution)/shard_map/reduce_scatter | solution.py:229
  1901.7 86.7 %all-to-all-start.8 = ((bf16[4,64,8192]{2,1,0:T(8,128)(2,1)}), bf16[4,64,8192]{2,1,0:T(8,128)(2,1)}, u32[]{:S(2)}, u32[]{:S(2)}) async-start(bf16[4,64,8192]{2,1,0:T(8,128)(2,1)} %bitcast.234), calls=%async_computation.9 | async-start | bytes 8388608 | tf_op jit(solution)/shard_map/all_to_all | solution.py:238
  1907.0 17.5 copy-start.3
  1907.0 17.5 copy-start.23
  1907.0 17.5 copy-start.27
  1924.5 13.8 copy-start.25
  1924.5 62.6 %copy-start.13 = (f32[128,2048]{1,0:T(8,128)S(1)}, f32[128,2048]{1,0:T(8,128)}, u32[]{:S(2)}) copy-start(f32[128,2048]{1,0:T(8,128)} %get-tuple-element.202) | copy-start | bytes 3145732
  (19 other events, 57.2 us)
Sparse Core Ops, SparseCore 0:
  9.8 230.2 all-gather.8
  242.0 87.4 all-gather.10
  331.4 576.6 all-gather.12
  909.8 297.0 all-gather.14
  1208.6 35.0 all-gather.18
  1274.2 51.1 all-gather.22
  1399.9 36.8 all-gather.20
  1453.8 61.1 all-gather.16
  1578.7 323.0 reduce-scatter.1
where the time goes:
time: 2010 us
  waiting for transfers between devices  1510 us (75%)
  matrix products  227 us (11%)
  local copies, waits for them, and re-layouts  99.7 us (5%)
  other arithmetic  55.9 us (3%)
  blocking collectives  47.7 us (2%)
  starting transfers between devices  41.8 us (2%)
    all_gather x1, waiting for transfers between devices, shards(): lax.all_gather(gate_up_weight, 'dp', axis=0, tiled=True)  541 us
    reduce_scatter x1, waiting for transfers between devices, shards(): lax.psum_scatter(jnp.concatenate([row_product(gathered_rows[which], split...  323 us
    all_gather x1, waiting for transfers between devices, shards(): lax.all_gather(down_weight, 'dp', axis=0, tiled=True)  264 us
    all_gather x1, waiting for transfers between devices, shards(): lax.all_gather(qkv_weight, 'dp', axis=0, tiled=True)  229 us
    all_to_all x2, waiting for transfers between devices, tokens_from_heads(): lax.all_to_all(flattened, 'seq', split_axis=0, concat_axis=2, tiled=True)  55.4 us
    dot_general x3, matrix products, keep_step(): running = jnp.dot(source, weight_piece, preferred_element_type=jnp.float32)  53.4 us
    all_to_all x2, waiting for transfers between devices, heads_from_tokens(): lax.all_to_all(token_block, 'seq', split_axis=2, concat_axis=0, tiled=True)  50.1 us
    unnamed x1, blocking collectives  47.7 us
  transfers between devices with their start and end apart: 18, of which 11 were waited for; matrix products, arithmetic and copies ran while one was open for 16% of the time, Pallas kernels for 0%

commit v1 on v0

--- a/solution.py
+++ b/solution.py
@@ -171,7 +171,10 @@
     sigmoid_gate = jax.nn.sigmoid(gate)
     act_low = (gate * sigmoid_gate * up_part).astype(jnp.bfloat16)
     mlp_out, down_full = keep_columns(
-        act_low, lax.all_gather(down_weight, "dp", axis=0, tiled=True)
+        act_low,
+        jnp.concatenate(
+            lax.all_to_all(jnp.stack([down_weight] * lax.axis_size("dp")), "dp", 0, 0), axis=0
+        ),
     )
     layer_out = hidden_res + mlp_out
     grad_low = cotangent.astype(jnp.bfloat16)

time: 2010 us -> 2090 us (1.040)
  waiting for transfers between devices: 1510 us -> 1560 us
  local copies, waits for them, and re-layouts: 99.7 us -> 121 us
    all_gather x1, waiting for transfers between devices: 541 us -> 865 us  [shards(): lax.all_gather(gate_up_weight, 'dp', axis=0, tiled=True)]
    all_gather x1 -> x0, waiting for transfers between devices: 264 us -> none  [shards(): lax.all_gather(down_weight, 'dp', axis=0, tiled=True)]
    all_to_all x2 -> x1, waiting for transfers between devices: 55.4 us -> 43.5 us  [tokens_from_heads(): lax.all_to_all(flattened, 'seq', split_axis=0, concat_axis=2, tiled=True)]
  transfers between devices with their start and end apart: 18 -> 17, of which waited for: 11 -> 9; matrix products, arithmetic and copies ran while one was open for 16% -> 16% of each run, Pallas kernels for 0% -> 0%
where the time goes in v1:
time: 2090 us
  waiting for transfers between devices  1560 us (75%)
  matrix products  218 us (10%)
  local copies, waits for them, and re-layouts  121 us (6%)
  blocking collectives  65.3 us (3%)
  other arithmetic  51.6 us (2%)
  starting transfers between devices  48.1 us (2%)
    all_gather x1, waiting for transfers between devices, shards(): lax.all_gather(gate_up_weight, 'dp', axis=0, tiled=True)  865 us
    reduce_scatter x1, waiting for transfers between devices, shards(): lax.psum_scatter(jnp.concatenate([row_product(gathered_rows[which], split...  323 us
    all_gather x1, waiting for transfers between devices, shards(): lax.all_gather(qkv_weight, 'dp', axis=0, tiled=True)  229 us
    all_to_all x2, waiting for transfers between devices, heads_from_tokens(): lax.all_to_all(token_block, 'seq', split_axis=2, concat_axis=0, tiled=True)  49.9 us
    unnamed x1, blocking collectives  47.6 us
    all_to_all x1, waiting for transfers between devices, tokens_from_heads(): lax.all_to_all(flattened, 'seq', split_axis=0, concat_axis=2, tiled=True)  43.5 us
    dot_general x3, matrix products, keep_step(): running = jnp.dot(source, weight_piece, preferred_element_type=jnp.float32)  42.9 us
  transfers between devices with their start and end apart: 17, of which 9 were waited for; matrix products, arithmetic and copies ran while one was open for 16% of the time, Pallas kernels for 0%

profile of v1, /device:TPU:0, one launch (start us, length us, event | category | flops | bytes accessed | tf_op | source)
XLA Modules:
  0.0 2085.2 jit_solution(8217282412140589770)
XLA Ops:
  10.7 229.4 %all-gather.8.cloned.1.call-done = bf16[2048,6144]{1,0:T(8,128)(2,1)} async-done(((bf16[512,6144]{1,0:T(8,128)(2,1)}), bf16[2048,6144]{1,0:T(8,128)(2,1)}) %all-gather.8.cloned.1.call-update) | async-done | bytes 25165840 | tf_op jit(solution)/shard_map/all_gather | solution.py:150
  240.2 11.6 convolution_convert_fusion.2
  260.0 36.3 %all-to-all-done = bf16[128,3,8,256]{3,0,1,2:T(8,128)(2,1)S(1)} async-done(((bf16[128,3,8,256]{3,0,1,2:T(8,128)(2,1)}), bf16[128,3,8,256]{3,0,1,2:T(8,128)(2,1)S(1)}, u32[]{:S(2)}, u32[]{:S(2)}) %all-to-all-start) | async-done | bytes 1572896 | tf_op jit(solution)/shard_map/all_to_all | solution.py:119
  303.8 17.7 while.27
  333.9 17.7 all_to_all.151
  351.7 19.7 stack.19
  371.3 9.8 all-to-all-start.2
  395.3 864.8 %all-gather.12.cloned.1.call-done = bf16[2048,16384]{1,0:T(8,128)(2,1)} async-done(((bf16[512,16384]{1,0:T(8,128)(2,1)}), bf16[2048,16384]{1,0:T(8,128)(2,1)}) %all-gather.12.cloned.1.call-update) | async-done | bytes 67108880 | tf_op jit(solution)/shard_map/all_gather | solution.py:167
  1260.1 26.6 %fusion.51 = f32[128,16384]{1,0:T(8,128)} fusion(bf16[128,2048]{1,0:T(8,128)(2,1)S(1)} %multiply_convert_fusion.4, bf16[2048,16384]{1,0:T(8,128)(2,1)} %all-gather.12.cloned.1.call-done), kind=kOutput, calls=%fused_computation.121 | convolution fusion | flops 8589934592 | bytes 76021760 | tf_op jit(solution)/shard_map/dot_general | solution.py:105
  1286.7 19.2 multiply_convert_fusion.2
  1305.8 30.5 %multiply_reduce_fusion = (f32[2048]{0:T(1024)}, f32[128]{0:T(128)S(1)}, f32[128,2048]{1,0:T(8,128)}) fusion(f32[128,2048]{1,0:T(8,128)S(1)} %copy-done.4, f32[128]{0:T(128)S(1)} %add_rsqrt_fusion, f32[2048]{0:T(1024)S(1)} %copy-done.29, bf16[2048,16384]{1,0:T(8,128)(2,1)} %all-gather.12.cloned.1.call-done, bf16[128,8192]{1,0:T(8,128)(2,1)} %get-tuple-element.206, ...), kind=kOutput, calls=%fused_computation.84 | convolution fusion | flops 8599894016 | bytes 73417728 | tf_op jit(solution)/shard_map/tc,rc->tr/dot_general | solution.py:185
  1339.2 6.3 convolution_convert_fusion.4
  1353.0 13.6 all-to-all-done.3
  1385.5 75.2 %while.28 = (s32[]{:T(128)}, f32[1024,4,64]{0,2,1:T(8,128)S(1)}, f32[1024,4,64]{0,2,1:T(8,128)}, f32[2,512,4,64]{1,0,3,2:T(2,128)}, s32[2]{0:T(128)S(1)}, /*inde...) while((s32[]{:T(128)}, f32[1024,4,64]{0,2,1:T(8,128)S(1)}, ...), condition=%wide.region_9.10_spmd.clone, body=%wide.region_8.9_spmd.clone.sunk | while | flops 1366819328 | bytes 69792104 | solution.py:93
  1393.8 5.8 multiply_convert_fusion.7
  1403.6 10.4 dynamic_update_slice.20
  1417.2 5.8 fusion.115
  1431.2 5.8 multiply_convert_fusion.7
  1441.0 10.4 dynamic_update_slice.20
  1454.6 6.1 fusion.115
  1481.9 43.5 %all-to-all-done.4 = bf16[1024,3,1,256]{3,1,2,0:T(4,128)(2,1)} async-done(((bf16[1024,3,1,256]{3,1,2,0:T(4,128)(2,1)}), bf16[1024,3,1,256]{3,1,2,0:T(4,128)(2,1)}, u32[]{:S(2)}, u32[]{:S(2)}) %all-to-all-start.4) | async-done | bytes 1572896 | tf_op jit(solution)/shard_map/all_to_all | solution.py:126
  1538.9 10.3 convert_bitcast_fusion.1
  1554.7 40.2 %all-to-all-done.7 = bf16[128,4,4096]{2,0,1:T(8,128)(2,1)} async-done(((bf16[128,4,4096]{2,0,1:T(8,128)(2,1)}), bf16[128,4,4096]{2,0,1:T(8,128)(2,1)}, u32[]{:S(2)}, u32[]{:S(2)}) %all-to-all-start.7) | async-done | bytes 4194336 | tf_op jit(solution)/shard_map/all_to_all | solution.py:229
  1599.6 14.9 convolution_convert_fusion
  1619.3 8.2 convolution_convert_fusion.1
  1627.5 8.7 copy.149
  1636.1 22.2 %pad_maximum_fusion = bf16[2048,8192]{1,0:T(8,128)(2,1)} fusion(bf16[2048,2048]{1,0:T(8,128)(2,1)} %convert_bitcast_fusion.1, bf16[2048,4096]{1,0:T(8,128)(2,1)} %convolution_convert_fusion, bf16[2048,512]{1,0:T(8,128)(2,1)S(1)} %copy.150, bf16[2048,1536]{1,0:T(8,128)(2,1)} %copy.149), kind=kLoop, calls=%fused_computation.43 | loop fusion | flops 134217728 | bytes 67108864 | tf_op jit(solution)/shard_map/concatenate | solution.py:233
  1658.4 323.2 %reduce-scatter.2.cloned.1.call-done = bf16[256,8192]{1,0:T(8,128)(2,1)} async-done(((bf16[2048,8192]{1,0:T(8,128)(2,1)}), bf16[256,8192]{1,0:T(8,128)(2,1)}) %reduce-scatter.2.cloned.1.call-update) | async-done | bytes 4194320 | tf_op jit(solution)/shard_map/reduce_scatter | solution.py:232
  1981.6 5.3 all-to-all-start.9
  1986.9 17.4 convolution_add_fusion
  2004.4 13.8 multiply_reduce_fusion.1
  2018.2 47.6 %all-reduce.2 = (f32[2048]{0:T(1024)S(1)}, f32[2048]{0:T(1024)S(1)}) all-reduce(f32[2048]{0:T(1024)S(1)} %get-tuple-element.159, f32[2048]{0:T(1024)S(1)} %copy-done.30), channel_id=2, replica_groups=mesh['dp'=4,'seq'=8] {'dp','seq'}, use_global_device_ids=true, to_apply=%region_12.13.clone | all-reduce | flops 4096 | bytes 32768
  (227 shorter events, 178.0 us)
Async XLA Ops:
  7.2 233.0 %all-gather.8.cloned.1.call-start = ((), (), s32[]{:S(2)}) async-start(), calls=%async_computation.11 | async-start | bytes 31457280 | tf_op jit(solution)/shard_map/all_gather | solution.py:150
  7.9 381.4 %all-gather.10.cloned.1.call-start = ((), (), s32[]{:S(2)}) async-start(), calls=%async_computation.12 | async-start | bytes 10485760 | tf_op jit(solution)/shard_map/all_gather | solution.py:161
  8.7 1251.4 %all-gather.12.cloned.1.call-start = ((), (), s32[]{:S(2)}) async-start(), calls=%async_computation.13 | async-start | bytes 83886080 | tf_op jit(solution)/shard_map/all_gather | solution.py:167
  10.7 241.0 %copy-start.9 = (bf16[128,2048]{1,0:T(8,128)(2,1)}, bf16[128,2048]{1,0:T(8,128)(2,1)S(1)}, u32[]{:S(2)}) copy-start(bf16[128,2048]{1,0:T(8,128)(2,1)S(1)} %multiply_convert_fusion.5) | copy-start | bytes 1572868
  253.7 42.6 %all-to-all-start = ((bf16[128,3,8,256]{3,0,1,2:T(8,128)(2,1)}), bf16[128,3,8,256]{3,0,1,2:T(8,128)(2,1)S(1)}, u32[]{:S(2)}, u32[]{:S(2)}) async-start(bf16[128,3,8,256]{3,0,1,2:T(8,128)(2,1)} %copy.121), calls=%async_computation | async-start | bytes 3145728 | tf_op jit(solution)/shard_map/all_to_all | solution.py:119
  259.1 43.0 %copy-start.13 = (f32[1024,64]{0,1:T(8,128)}, f32[1024,64]{0,1:T(8,128)S(1)}, u32[]{:S(2)}) copy-start(f32[1024,64]{0,1:T(8,128)S(1)} %pad_maximum_fusion.4) | copy-start | bytes 786436
  371.3 915.3 %all-to-all-start.2 = ((bf16[4,512,8192]{2,1,0:T(8,128)(2,1)}), bf16[4,512,8192]{2,1,0:T(8,128)(2,1)}, u32[]{:S(2)}, u32[]{:S(2)}) async-start(bf16[4,512,8192]{2,1,0:T(8,128)(2,1)} %stack.19), calls=%async_computation.2 | async-start | bytes 67108864 | tf_op jit(solution)/shard_map/all_to_all | solution.py:176
  381.2 1150.5 %all-gather.16.cloned.1.call-start = ((), (), s32[]{:S(2)}) async-start(), calls=%async_computation.15 | async-start | bytes 2621440 | tf_op jit(solution)/shard_map/all_gather | solution.py:216
  383.2 903.5 %copy-start.23 = (bf16[128,2048]{0,1:T(8,128)(2,1)}, bf16[128,2048]{0,1:T(8,128)(2,1)S(1)}, u32[]{:S(2)}) copy-start(bf16[128,2048]{0,1:T(8,128)(2,1)S(1)} %copy.126) | copy-start | bytes 1572868
  395.2 891.4 %copy-start.11 = (bf16[128,2048]{1,0:T(8,128)(2,1)}, bf16[128,2048]{1,0:T(8,128)(2,1)S(1)}, u32[]{:S(2)}) copy-start(bf16[128,2048]{1,0:T(8,128)(2,1)S(1)} %multiply_convert_fusion.4) | copy-start | bytes 1572868
  1286.6 19.2 copy-start.4
  1339.2 12.0 copy-start.24
  1345.5 25.2 %copy-start.20 = (bf16[2,512,4,64]{1,3,2,0:T(8,128)(2,1)S(1)}, bf16[2,512,4,64]{1,3,2,0:T(8,128)(2,1)}, u32[]{:S(2)}) copy-start(bf16[2,512,4,64]{1,3,2,0:T(8,128)(2,1)} %get-tuple-element.105) | copy-start | bytes 1572868
  1346.6 20.0 all-to-all-start.3
  1351.1 187.7 %all-gather.20.cloned.1.call-start = ((), (), s32[]{:S(2)}) async-start(), calls=%async_computation.17 | async-start | bytes 2621440 | tf_op jit(solution)/shard_map/all_gather | solution.py:222
  1366.6 14.3 all-to-all-start.6
  1380.9 91.1 %all-to-all-start.8 = ((bf16[128,4,2048]{2,0,1:T(8,128)(2,1)}), bf16[128,4,2048]{2,0,1:T(8,128)(2,1)}, u32[]{:S(2)}, u32[]{:S(2)}) async-start(bf16[128,4,2048]{2,0,1:T(8,128)(2,1)} %bitcast.226), calls=%async_computation.8 | async-start | bytes 4194304 | tf_op jit(solution)/shard_map/all_to_all | solution.py:230
  1385.5 8.3 copy-start.21
  1423.0 8.3 copy-start.21
  1472.0 53.4 %all-to-all-start.4 = ((bf16[1024,3,1,256]{3,1,2,0:T(4,128)(2,1)}), bf16[1024,3,1,256]{3,1,2,0:T(4,128)(2,1)}, u32[]{:S(2)}, u32[]{:S(2)}) async-start(bf16[1024,3,1,256]{3,1,2,0:T(4,128)(2,1)} %copy.132), calls=%async_computation.4 | async-start | bytes 4194304 | tf_op jit(solution)/shard_map/all_to_all | solution.py:126
  1476.3 123.2 %all-gather.18.cloned.1.call-start = ((), (), s32[]{:S(2)}) async-start(), calls=%async_computation.16 | async-start | bytes 2621440 | tf_op jit(solution)/shard_map/all_gather | solution.py:219
  1481.9 48.6 %copy-start.10 = (bf16[128,2048]{1,0:T(8,128)(2,1)S(1)}, bf16[128,2048]{1,0:T(8,128)(2,1)}, u32[]{:S(2)}) copy-start(bf16[128,2048]{1,0:T(8,128)(2,1)} %copy-done.9) | copy-start | bytes 1572868
  1525.3 69.6 %all-to-all-start.7 = ((bf16[128,4,4096]{2,0,1:T(8,128)(2,1)}), bf16[128,4,4096]{2,0,1:T(8,128)(2,1)}, u32[]{:S(2)}, u32[]{:S(2)}) async-start(bf16[128,4,4096]{2,0,1:T(8,128)(2,1)} %pad_maximum_fusion.1), calls=%async_computation.7 | async-start | bytes 8388608 | tf_op jit(solution)/shard_map/all_to_all | solution.py:229
  1530.4 88.8 %all-gather.14.cloned.1.call-start = ((), (), s32[]{:S(2)}) async-start(), calls=%async_computation.14 | async-start | bytes 2621440 | tf_op jit(solution)/shard_map/all_gather | solution.py:213
  1594.9 21.8 %all-to-all-start.5 = ((bf16[128,4,1536]{0,2,1:T(8,128)(2,1)}), bf16[128,4,1536]{0,2,1:T(8,128)(2,1)}, u32[]{:S(2)}, u32[]{:S(2)}) async-start(bf16[128,4,1536]{0,2,1:T(8,128)(2,1)} %bitcast.31), calls=%async_computation.5 | async-start | bytes 3145728 | tf_op jit(solution)/shard_map/all_to_all | solution.py:227
  1599.2 382.3 %reduce-scatter.2.cloned.1.call-start = ((), (), s32[]{:S(2)}) async-start(), calls=%async_computation.18 | async-start | bytes 37748736 | tf_op jit(solution)/shard_map/reduce_scatter | solution.py:232
  1981.6 86.7 %all-to-all-start.9 = ((bf16[4,64,8192]{2,1,0:T(8,128)(2,1)}), bf16[4,64,8192]{2,1,0:T(8,128)(2,1)}, u32[]{:S(2)}, u32[]{:S(2)}) async-start(bf16[4,64,8192]{2,1,0:T(8,128)(2,1)} %bitcast.236), calls=%async_computation.10 | async-start | bytes 8388608 | tf_op jit(solution)/shard_map/all_to_all | solution.py:241
  1986.9 17.5 copy-start.2
  1986.9 17.5 copy-start.28
  1986.9 17.5 copy-start.32
  2004.3 13.8 copy-start.30
  2004.4 62.6 %copy-start.15 = (f32[128,2048]{1,0:T(8,128)S(1)}, f32[128,2048]{1,0:T(8,128)}, u32[]{:S(2)}) copy-start(f32[128,2048]{1,0:T(8,128)} %get-tuple-element.202) | copy-start | bytes 3145732
  (24 other events, 56.4 us)
Sparse Core Ops, SparseCore 0:
  9.8 230.2 all-gather.7
  242.0 87.4 all-gather.9
  331.4 928.6 all-gather.11
  1261.7 35.0 all-gather.15
  1353.5 51.6 all-gather.19
  1479.2 36.8 all-gather.17
  1533.7 61.1 all-gather.13
  1658.5 323.0 reduce-scatter.1
